TPU v7x, 128 devices: a whole 4x4x4 slice. The times are simulated.
128 devices in a mesh: loop: 32 (over y, x, z_lo), cross: 4 (over z_hi, core).
Axes of the slice: x: 4, y: 4, z: 4 (z_hi: 2, z_lo: 2; z = z_hi * 2 + z_lo), core: 2. Of those that a mesh axis runs over, the one named last changes fastest.
Arguments:
- populations: float32 [27, 256, 128, 128], P(None, 'loop', 'cross'), may hold values from 0 to 1, as said below
- scalars: float32 [14, 256, 128, 128], P(None, 'loop', 'cross'), may hold values from 0 to 1, as said below
- node_flags: int32 [256, 128, 128], P('loop', 'cross'), may hold values from 0 to 4, as said below
Outputs:
- new_populations: float32 [27, 256, 128, 128], P(None, 'loop', 'cross')
- new_scalars: float32 [14, 256, 128, 128], P(None, 'loop', 'cross')
Inputs may be any that keep to these rules, and one draw needn't show every extreme that they name: `node_flags`: every cell in the first or last layer along either cross-section dimension is a wall. `populations`: all entries positive. `scalars`: all entries positive.
All inputs are finite; a program needn't handle non-finite values.
Results may differ from a plain program's by a relative error of at most 0.0001.
Values sent between devices are 32-bit elements; how exact they have to be, the bound alone decides.
A program may use at most 128 MiB of HBM per device.

v0:
```python
import jax
import jax.numpy as jnp
from jax import lax
from jax.sharding import PartitionSpec as P

relax_flow = 0.8
relax_heat = 0.9
relax_solvent = 1.1
fan_speed = 0.05
heater_temp = 2.0


def padded_2(cells, sides, width, closed):
    for axis, dim in sides:
        count = lax.axis_size(axis)
        ends = count if closed else count - 1
        head = lax.slice_in_dim(cells, 0, width, axis=dim)
        tail = lax.slice_in_dim(cells, cells.shape[dim] - width, cells.shape[dim], axis=dim)
        cells = jnp.concatenate(
            [
                lax.ppermute(tail, axis, [(i, (i + 1) % count) for i in range(ends)]),
                cells,
                lax.ppermute(head, axis, [((i + 1) % count, i) for i in range(ends)]),
            ],
            axis=dim,
        )
    return cells


def flow_dirs():
    return [(a, b, c) for a in (-1, 0, 1) for b in (-1, 0, 1) for c in (-1, 0, 1)]


def flow_weights():
    table = {0: 8.0 / 27.0, 1: 2.0 / 27.0, 2: 1.0 / 54.0, 3: 1.0 / 216.0}
    return [table[abs(a) + abs(b) + abs(c)] for a, b, c in flow_dirs()]


def scalar_dirs():
    return [(0, 0, 0), (1, 0, 0), (-1, 0, 0), (0, 1, 0), (0, -1, 0), (0, 0, 1), (0, 0, -1)]


def scalar_opposite():
    return [0, 2, 1, 4, 3, 6, 5]


def scalar_weights():
    return [0.25, 0.125, 0.125, 0.125, 0.125, 0.125, 0.125]


def state_dirs():
    return flow_dirs() + scalar_dirs() + scalar_dirs()


def collide(pops, scal, flags):
    flow = flow_dirs()
    weights = flow_weights()
    wall = flags == 1
    fan = flags == 2
    heater = flags == 3
    exhaust = flags == 4
    density = jnp.sum(pops, axis=0)
    denom = jnp.where(wall, 1.0, density)
    table = jnp.array(flow, dtype=jnp.float32)
    mom_x = jnp.sum(pops * table[:, 0][:, None, None, None], axis=0)
    mom_y = jnp.sum(pops * table[:, 1][:, None, None, None], axis=0)
    mom_z = jnp.sum(pops * table[:, 2][:, None, None, None], axis=0)
    vel_x = jnp.where(fan, fan_speed, mom_x / denom)
    vel_y = jnp.where(fan, 0.0, mom_y / denom)
    vel_z = jnp.where(fan, 0.0, mom_z / denom)
    rho_eq = jnp.where(exhaust, 1.0, density)
    usq = vel_x * vel_x + vel_y * vel_y + vel_z * vel_z
    out_flow = []
    for index, (a, b, c) in enumerate(flow):
        proj = a * vel_x + b * vel_y + c * vel_z
        feq = weights[index] * rho_eq * (1.0 + 3.0 * proj + 4.5 * proj * proj - 1.5 * usq)
        relaxed = pops[index] - (pops[index] - feq) / relax_flow
        forced = jnp.where(fan | exhaust, feq, relaxed)
        out_flow.append(jnp.where(wall, pops[26 - index], forced))
    temp = jnp.sum(scal[0:7], axis=0)
    solv = jnp.sum(scal[7:14], axis=0)
    heat_out = []
    solv_out = []
    opposite = scalar_opposite()
    sweights = scalar_weights()
    for index, (a, b, c) in enumerate(scalar_dirs()):
        proj = a * vel_x + b * vel_y + c * vel_z
        factor = 1.0 + 4.0 * proj
        geq = sweights[index] * temp * factor
        hot = sweights[index] * heater_temp * factor
        relaxed = scal[index] - (scal[index] - geq) / relax_heat
        heat_out.append(jnp.where(wall, scal[opposite[index]], jnp.where(heater, hot, relaxed)))
        heq = sweights[index] * solv * factor
        relaxed = scal[7 + index] - (scal[7 + index] - heq) / relax_solvent
        solv_out.append(
            jnp.where(wall, scal[7 + opposite[index]], jnp.where(exhaust, 0.0, relaxed))
        )
    return (jnp.stack(out_flow), jnp.stack(heat_out + solv_out))


def shift_block(wide, size_x, size_y):
    padded = jnp.pad(wide, ((0, 0), (0, 0), (0, 0), (1, 1)))
    size_z = wide.shape[3]
    result = []
    for index, (a, b, c) in enumerate(state_dirs()):
        result.append(
            padded[index, 1 - a : 1 - a + size_x, 1 - b : 1 - b + size_y, 1 - c : 1 - c + size_z]
        )
    return jnp.stack(result)


def extend_once(post):
    wide = padded_2(post, (("loop", 1),), 1, True)
    return padded_2(wide, (("cross", 2),), 1, False)


def per_device(populations, scalars, node_flags):
    size_x = node_flags.shape[0]
    size_y = node_flags.shape[1]
    fields = jnp.concatenate([populations, scalars], axis=0)
    for step in range(2):
        post_flow, post_scal = collide(fields[:27], fields[27:], node_flags)
        post = jnp.concatenate([post_flow, post_scal], axis=0)
        fields = shift_block(extend_once(post), size_x, size_y)
    return (fields[:27], fields[27:])


def solution(mesh):
    in_specs = (
        P(None, "loop", "cross", None),
        P(None, "loop", "cross", None),
        P("loop", "cross", None),
    )
    out_specs = (P(None, "loop", "cross", None), P(None, "loop", "cross", None))
    return jax.shard_map(
        per_device, mesh=mesh, in_specs=in_specs, out_specs=out_specs, check_vma=False
    )
```

profile of v0, /device:TPU:1, one launch (start us, length us, event | category | flops | bytes accessed | tf_op | source)
XLA Modules:
  0.0 131.7 jit_solution(8347659003404394776)
XLA Ops:
  0.7 1.8 %slice_reduce_fusion = (f32[8,32,128]{2,1,0:T(8,128)S(1)}, f32[8,32,128]{2,1,0:T(8,128)S(1)}) fusion(f32[14,8,32,128]{3,2,1,0:T(8,128)} %param.6), kind=kLoop, calls=%fused_computation.17 | loop fusion | flops 393216 | bytes 2097152 | tf_op jit(solution)/shard_map/reduce_sum | solution.py:81
  2.5 3.0 %multiply_reduce_fusion.5 = (f32[8,32,128]{2,1,0:T(8,128)S(1)}, f32[8,32,128]{2,1,0:T(8,128)S(1)}, f32[8,32,128]{2,1,0:T(8,128)S(1)}, f32[8,32,128]{2,1,0:T(8,128)S(1)}) fusion(f32[27,8,32,128]{3,2,1,0:T(8,128)} %param.5, f32[27]{0:T(128)} %constant.141, f32[27]{0:T(128)} %constant.145, f32[27]{0:T(128)} %constant.143), kind=kLoop, calls=%fused_computation.16 | loop fusion | flops 6062080 | bytes 4063556 | tf_op jit(solution)/shard_map/reduce_sum | solution.py:65
  5.5 0.2 constant_dynamic-update-slice_fusion.40
  5.7 0.1 constant_dynamic-update-slice_fusion.39
  5.8 0.1 constant_dynamic-update-slice_fusion.38
  6.0 0.1 constant_dynamic-update-slice_fusion.37
  6.3 0.1 constant_dynamic-update-slice_fusion.34
  6.4 0.1 constant_dynamic-update-slice_fusion.33
  6.5 0.1 constant_dynamic-update-slice_fusion.32
  6.6 0.1 constant_dynamic-update-slice_fusion.31
  7.0 0.1 constant_dynamic-update-slice_fusion.28
  7.3 0.1 constant_dynamic-update-slice_fusion.25
  7.6 0.1 constant_dynamic-update-slice_fusion.22
  7.7 0.1 constant_dynamic-update-slice_fusion.21
  7.9 0.1 constant_dynamic-update-slice_fusion.20
  8.0 0.1 constant_dynamic-update-slice_fusion.19
  8.6 0.4 copy-done.1
  10.3 2.5 %collective-permute-start = (f32[41,1,32,128]{3,2,1,0:T(8,128)S(1)}, f32[41,1,32,128]{3,2,1,0:T(8,128)S(1)}, u32[]{:S(2)}, u32[]{:S(2)}) collective-permute-start(f32[41,1,32,128]{3,2,1,0:T(8,128)S(1)} %get-tuple-element.110), channel_id=1, source_target_pairs={{0,4},{4,8},{8,12},{12,16},{16,20},{20,24},{24,28},{28,32},{32,36}... | collective-permute-start | bytes 2015240 | tf_op jit(solution)/shard_map/ppermute | solution.py:21
  12.9 4.7 %collective-permute-start.1 = (f32[41,1,32,128]{3,2,1,0:T(8,128)S(1)}, f32[41,1,32,128]{3,2,1,0:T(8,128)S(1)}, u32[]{:S(2)}, u32[]{:S(2)}) collective-permute-start(f32[41,1,32,128]{3,2,1,0:T(8,128)S(1)} %get-tuple-element.111), channel_id=1, source_target_pairs={{4,0},{8,4},{12,8},{16,12},{20,16},{24,20},{28,24},{32,28},{36,32}... | collective-permute-start | bytes 2015240 | tf_op jit(solution)/shard_map/ppermute | solution.py:23
  17.6 23.4 %collective-permute-done = f32[41,1,32,128]{3,2,1,0:T(8,128)S(1)} collective-permute-done((f32[41,1,32,128]{3,2,1,0:T(8,128)S(1)}, f32[41,1,32,128]{3,2,1,0:T(8,128)S(1)}, u32[]{:S(2)}, u32[]{:S(2)}) %collective-permute-start) | collective-permute-done | bytes 671776 | tf_op jit(solution)/shard_map/ppermute | solution.py:21
  41.0 1.9 %collective-permute-done.1 = f32[41,1,32,128]{3,2,1,0:T(8,128)S(1)} collective-permute-done((f32[41,1,32,128]{3,2,1,0:T(8,128)S(1)}, f32[41,1,32,128]{3,2,1,0:T(8,128)S(1)}, u32[]{:S(2)}, u32[]{:S(2)}) %collective-permute-start.1) | collective-permute-done | bytes 671776 | tf_op jit(solution)/shard_map/ppermute | solution.py:23
  42.9 0.3 pad_maximum_fusion.5
  43.2 7.0 %collective-permute-start.2 = (f32[41,10,1,128]{3,2,1,0:T(1,128)S(1)}, f32[41,10,1,128]{3,2,1,0:T(1,128)S(1)}, u32[]{:S(2)}, u32[]{:S(2)}) collective-permute-start(f32[41,10,1,128]{3,2,1,0:T(1,128)S(1)} %get-tuple-element.102), channel_id=1, source_target_pairs={{0,1},{1,2},{2,3},{4,5},{5,6},{6,7},{8,9},{9,10},{10,11},{12,13},{... | collective-permute-start | bytes 629768 | tf_op jit(solution)/shard_map/ppermute | solution.py:21
  50.2 2.1 %collective-permute-start.3 = (f32[41,10,1,128]{3,2,1,0:T(1,128)S(1)}, f32[41,10,1,128]{3,2,1,0:T(1,128)S(1)}, u32[]{:S(2)}, u32[]{:S(2)}) collective-permute-start(f32[41,10,1,128]{3,2,1,0:T(1,128)S(1)} %get-tuple-element.103), channel_id=1, source_target_pairs={{1,0},{2,1},{3,2},{5,4},{6,5},{7,6},{9,8},{10,9},{11,10},{13,12},{... | collective-permute-start | bytes 629768 | tf_op jit(solution)/shard_map/ppermute | solution.py:23
  52.3 0.6 collective-permute-done.2
  52.9 5.9 %collective-permute-done.3 = f32[41,10,1,128]{3,2,1,0:T(1,128)S(1)} collective-permute-done((f32[41,10,1,128]{3,2,1,0:T(1,128)S(1)}, f32[41,10,1,128]{3,2,1,0:T(1,128)S(1)}, u32[]{:S(2)}, u32[]{:S(2)}) %collective-permute-start.3) | collective-permute-done | bytes 209952 | tf_op jit(solution)/shard_map/ppermute | solution.py:23
  58.8 11.4 %select_maximum_fusion.4 = f32[41,10,34,130]{3,2,1,0:T(8,128)S(1)} fusion(f32[41,10,1,128]{3,2,1,0:T(1,128)S(1)} %collective-permute-done.3, f32[41,10,1,128]{3,2,1,0:T(1,128)S(1)} %collective-permute-done.2, f32[41,1,32,128]{3,2,1,0:T(8,128)S(1)} %collective-permute-done.1, f32[41,8,32,128]{3,2,1,0:T(8,128)S(1)} %constant_dynamic-update-slice_fusion, ...), kind=kLoop, calls=%fused_computation.6 | loop fusion | flops 21746400 | bytes 14386080 | tf_op jit(solution)/shard_map/concatenate | solution.py:19
  71.6 0.4 copy-done.5
  72.1 0.9 multiply_reduce_fusion.2
  73.0 0.6 constant_dynamic-update-slice_fusion.149
  73.7 0.2 constant_dynamic-update-slice_fusion.108
  74.0 0.1 constant_dynamic-update-slice_fusion.106
  74.1 0.1 constant_dynamic-update-slice_fusion.105
  74.3 0.1 constant_dynamic-update-slice_fusion.103
  74.5 0.1 constant_dynamic-update-slice_fusion.102
  74.7 0.1 constant_dynamic-update-slice_fusion.100
  74.9 0.1 constant_dynamic-update-slice_fusion.99
  75.1 0.1 constant_dynamic-update-slice_fusion.97
  75.2 0.1 constant_dynamic-update-slice_fusion.96
  75.5 0.1 constant_dynamic-update-slice_fusion.94
  75.6 0.1 constant_dynamic-update-slice_fusion.93
  75.8 0.1 constant_dynamic-update-slice_fusion.91
  76.0 0.1 constant_dynamic-update-slice_fusion.90
  76.2 0.1 constant_dynamic-update-slice_fusion.88
  76.3 0.1 constant_dynamic-update-slice_fusion.87
  76.6 0.1 constant_dynamic-update-slice_fusion.85
  76.7 0.1 constant_dynamic-update-slice_fusion.84
  77.0 0.1 constant_dynamic-update-slice_fusion.82
  77.6 0.1 constant_dynamic-update-slice_fusion.75
  77.7 0.2 constant_dynamic-update-slice_fusion.74
  78.3 0.1 constant_dynamic-update-slice_fusion.68
  78.6 5.7 %collective-permute-start.5 = (f32[41,1,32,128]{3,2,1,0:T(8,128)S(1)}, f32[41,1,32,128]{3,2,1,0:T(8,128)S(1)}, u32[]{:S(2)}, u32[]{:S(2)}) collective-permute-start(f32[41,1,32,128]{3,2,1,0:T(8,128)S(1)} %get-tuple-element.109), channel_id=1, source_target_pairs={{4,0},{8,4},{12,8},{16,12},{20,16},{24,20},{28,24},{32,28},{36,32}... | collective-permute-start | bytes 2015240 | tf_op jit(solution)/shard_map/ppermute | solution.py:23
  84.3 18.5 %collective-permute-done.4 = f32[41,1,32,128]{3,2,1,0:T(8,128)S(1)} collective-permute-done((f32[41,1,32,128]{3,2,1,0:T(8,128)S(1)}, f32[41,1,32,128]{3,2,1,0:T(8,128)S(1)}, u32[]{:S(2)}, u32[]{:S(2)}) %collective-permute-start.4) | collective-permute-done | bytes 671776 | tf_op jit(solution)/shard_map/ppermute | solution.py:21
  102.8 2.7 %collective-permute-done.5 = f32[41,1,32,128]{3,2,1,0:T(8,128)S(1)} collective-permute-done((f32[41,1,32,128]{3,2,1,0:T(8,128)S(1)}, f32[41,1,32,128]{3,2,1,0:T(8,128)S(1)}, u32[]{:S(2)}, u32[]{:S(2)}) %collective-permute-start.5) | collective-permute-done | bytes 671776 | tf_op jit(solution)/shard_map/ppermute | solution.py:23
  105.5 0.3 pad_maximum_fusion.2
  105.8 1.9 %collective-permute-start.7 = (f32[41,10,1,128]{3,0,2,1:T(8,128)S(1)}, f32[41,10,1,128]{3,0,2,1:T(8,128)S(1)}, u32[]{:S(2)}, u32[]{:S(2)}) collective-permute-start(f32[41,10,1,128]{3,0,2,1:T(8,128)S(1)} %copy.53), channel_id=1, source_target_pairs={{1,0},{2,1},{3,2},{5,4},{6,5},{7,6},{9,8},{10,9},{11,10},{13,12},{... | collective-permute-start | bytes 629768 | tf_op jit(solution)/shard_map/ppermute | solution.py:23
  107.8 5.4 %collective-permute-start.6 = (f32[41,10,1,128]{3,0,2,1:T(8,128)S(1)}, f32[41,10,1,128]{3,0,2,1:T(8,128)S(1)}, u32[]{:S(2)}, u32[]{:S(2)}) collective-permute-start(f32[41,10,1,128]{3,0,2,1:T(8,128)S(1)} %copy.52), channel_id=1, source_target_pairs={{0,1},{1,2},{2,3},{4,5},{5,6},{6,7},{8,9},{9,10},{10,11},{12,13},{... | collective-permute-start | bytes 629768 | tf_op jit(solution)/shard_map/ppermute | solution.py:21
  113.2 1.7 %collective-permute-done.7 = f32[41,10,1,128]{3,0,2,1:T(8,128)S(1)} collective-permute-done((f32[41,10,1,128]{3,0,2,1:T(8,128)S(1)}, f32[41,10,1,128]{3,0,2,1:T(8,128)S(1)}, u32[]{:S(2)}, u32[]{:S(2)}) %collective-permute-start.7) | collective-permute-done | bytes 209952 | tf_op jit(solution)/shard_map/ppermute | solution.py:23
  114.8 0.2 copy.55
  115.1 1.0 collective-permute-done.6
  116.1 0.2 copy.54
  116.3 11.4 %select_maximum_fusion = f32[41,10,34,130]{3,2,1,0:T(8,128)S(1)} fusion(f32[41,10,1,128]{3,2,1,0:T(1,128)S(1)} %copy.55, f32[41,10,1,128]{3,2,1,0:T(1,128)S(1)} %copy.54, f32[41,1,32,128]{3,2,1,0:T(8,128)S(1)} %collective-permute-done.5, f32[41,8,32,128]{3,2,1,0:T(8,128)S(1)} %constant_dynamic-update-slice_fusion.68, ...), kind=kLoop, calls=%fused_computation.2 | loop fusion | flops 21746400 | bytes 14386080 | tf_op jit(solution)/shard_map/concatenate | solution.py:19
  129.4 1.2 copy-done.3
  130.6 1.2 copy-done.4
  (123 shorter events, 7.3 us)
Async XLA Ops:
  0.6 4.9 %copy-start = (f32[27,8,32,128]{3,2,1,0:T(8,128)S(1)}, f32[27,8,32,128]{3,2,1,0:T(8,128)}, u32[]{:S(2)}) copy-start(f32[27,8,32,128]{3,2,1,0:T(8,128)} %param.5) | copy-start | bytes 10616836
  0.6 4.9 %copy-start.2 = (s32[8,32,128]{2,1,0:T(8,128)S(1)}, s32[8,32,128]{2,1,0:T(8,128)}, u32[]{:S(2)}) copy-start(s32[8,32,128]{2,1,0:T(8,128)} %param.7) | copy-start | bytes 393220
  7.5 1.5 %copy-start.1 = (f32[14,8,32,128]{3,2,1,0:T(8,128)S(1)}, f32[14,8,32,128]{3,2,1,0:T(8,128)}, u32[]{:S(2)}) copy-start(f32[14,8,32,128]{3,2,1,0:T(8,128)} %param.6) | copy-start | bytes 5505028
  10.3 30.7 %collective-permute-start = (f32[41,1,32,128]{3,2,1,0:T(8,128)S(1)}, f32[41,1,32,128]{3,2,1,0:T(8,128)S(1)}, u32[]{:S(2)}, u32[]{:S(2)}) collective-permute-start(f32[41,1,32,128]{3,2,1,0:T(8,128)S(1)} %get-tuple-element.110), channel_id=1, source_target_pairs={{0,4},{4,8},{8,12},{12,16},{16,20},{20,24},{24,28},{28,32},{32,36}... | collective-permute-start | bytes 2015240 | tf_op jit(solution)/shard_map/ppermute | solution.py:21
  12.9 30.0 %collective-permute-start.1 = (f32[41,1,32,128]{3,2,1,0:T(8,128)S(1)}, f32[41,1,32,128]{3,2,1,0:T(8,128)S(1)}, u32[]{:S(2)}, u32[]{:S(2)}) collective-permute-start(f32[41,1,32,128]{3,2,1,0:T(8,128)S(1)} %get-tuple-element.111), channel_id=1, source_target_pairs={{4,0},{8,4},{12,8},{16,12},{20,16},{24,20},{28,24},{32,28},{36,32}... | collective-permute-start | bytes 2015240 | tf_op jit(solution)/shard_map/ppermute | solution.py:23
  43.2 9.7 %collective-permute-start.2 = (f32[41,10,1,128]{3,2,1,0:T(1,128)S(1)}, f32[41,10,1,128]{3,2,1,0:T(1,128)S(1)}, u32[]{:S(2)}, u32[]{:S(2)}) collective-permute-start(f32[41,10,1,128]{3,2,1,0:T(1,128)S(1)} %get-tuple-element.102), channel_id=1, source_target_pairs={{0,1},{1,2},{2,3},{4,5},{5,6},{6,7},{8,9},{9,10},{10,11},{12,13},{... | collective-permute-start | bytes 629768 | tf_op jit(solution)/shard_map/ppermute | solution.py:21
  50.2 8.6 %collective-permute-start.3 = (f32[41,10,1,128]{3,2,1,0:T(1,128)S(1)}, f32[41,10,1,128]{3,2,1,0:T(1,128)S(1)}, u32[]{:S(2)}, u32[]{:S(2)}) collective-permute-start(f32[41,10,1,128]{3,2,1,0:T(1,128)S(1)} %get-tuple-element.103), channel_id=1, source_target_pairs={{1,0},{2,1},{3,2},{5,4},{6,5},{7,6},{9,8},{10,9},{11,10},{13,12},{... | collective-permute-start | bytes 629768 | tf_op jit(solution)/shard_map/ppermute | solution.py:23
  71.4 0.7 copy-start.5
  71.4 0.7 copy-start.6
  71.4 0.7 copy-start.7
  78.6 24.3 %collective-permute-start.4 = (f32[41,1,32,128]{3,2,1,0:T(8,128)S(1)}, f32[41,1,32,128]{3,2,1,0:T(8,128)S(1)}, u32[]{:S(2)}, u32[]{:S(2)}) collective-permute-start(f32[41,1,32,128]{3,2,1,0:T(8,128)S(1)} %get-tuple-element.108), channel_id=1, source_target_pairs={{0,4},{4,8},{8,12},{12,16},{16,20},{20,24},{24,28},{28,32},{32,36}... | collective-permute-start | bytes 2015240 | tf_op jit(solution)/shard_map/ppermute | solution.py:21
  78.6 26.9 %collective-permute-start.5 = (f32[41,1,32,128]{3,2,1,0:T(8,128)S(1)}, f32[41,1,32,128]{3,2,1,0:T(8,128)S(1)}, u32[]{:S(2)}, u32[]{:S(2)}) collective-permute-start(f32[41,1,32,128]{3,2,1,0:T(8,128)S(1)} %get-tuple-element.109), channel_id=1, source_target_pairs={{4,0},{8,4},{12,8},{16,12},{20,16},{24,20},{28,24},{32,28},{36,32}... | collective-permute-start | bytes 2015240 | tf_op jit(solution)/shard_map/ppermute | solution.py:23
  105.8 9.0 %collective-permute-start.7 = (f32[41,10,1,128]{3,0,2,1:T(8,128)S(1)}, f32[41,10,1,128]{3,0,2,1:T(8,128)S(1)}, u32[]{:S(2)}, u32[]{:S(2)}) collective-permute-start(f32[41,10,1,128]{3,0,2,1:T(8,128)S(1)} %copy.53), channel_id=1, source_target_pairs={{1,0},{2,1},{3,2},{5,4},{6,5},{7,6},{9,8},{10,9},{11,10},{13,12},{... | collective-permute-start | bytes 629768 | tf_op jit(solution)/shard_map/ppermute | solution.py:23
  107.8 8.3 %collective-permute-start.6 = (f32[41,10,1,128]{3,0,2,1:T(8,128)S(1)}, f32[41,10,1,128]{3,0,2,1:T(8,128)S(1)}, u32[]{:S(2)}, u32[]{:S(2)}) collective-permute-start(f32[41,10,1,128]{3,0,2,1:T(8,128)S(1)} %copy.52), channel_id=1, source_target_pairs={{0,1},{1,2},{2,3},{4,5},{5,6},{6,7},{8,9},{9,10},{10,11},{12,13},{... | collective-permute-start | bytes 629768 | tf_op jit(solution)/shard_map/ppermute | solution.py:21
  129.3 1.2 copy-start.3
  129.4 2.4 %copy-start.4 = (f32[27,8,32,128]{3,2,1,0:T(8,128)}, f32[27,8,32,128]{3,2,1,0:T(8,128)S(1)}, u32[]{:S(2)}) copy-start(f32[27,8,32,128]{3,2,1,0:T(8,128)S(1)} %get-tuple-element.89) | copy-start | bytes 10616836
where the time goes:
time: 132 us
  waiting for transfers between devices  55.7 us (42%)
  other arithmetic  38.9 us (29%)
  starting transfers between devices  29.4 us (22%)
  local copies, waits for them, and re-layouts  6.18 us (5%)
  between operations  1.58 us (1%)
    ppermute x4, waiting for transfers between devices, padded_2(): lax.ppermute(tail, axis, [(i, (i + 1) % count) for i in range(ends)])  43.6 us
    concatenate x2, other arithmetic, padded_2(): jnp.concatenate([lax.ppermute(tail, axis, [(i, (i + 1) % count) for i in...  22.8 us
    ppermute x4, starting transfers between devices, padded_2(): lax.ppermute(tail, axis, [(i, (i + 1) % count) for i in range(ends)])  14.9 us
    ppermute x4, starting transfers between devices, padded_2(): lax.ppermute(head, axis, [((i + 1) % count, i) for i in range(ends)])  14.4 us
    ppermute x4, waiting for transfers between devices, padded_2(): lax.ppermute(head, axis, [((i + 1) % count, i) for i in range(ends)])  12.1 us
    unnamed x100, other arithmetic  9.62 us
    unnamed x54, local copies, waits for them, and re-layouts  5.38 us
    reduce_sum x2, other arithmetic, collide(): mom_x = jnp.sum(pops * table[:, 0][:, None, None, None], axis=0)  3.92 us
  transfers between devices with their start and end apart: 8, of which 8 were waited for; matrix products, arithmetic and copies ran while one was open for 0% of the time, Pallas kernels for 0%

commit v1 on v0

v1 whole, which is shorter than its diff:
```python
import functools

import jax
import jax.numpy as jnp
from jax import lax
from jax.experimental import pallas as pl
from jax.experimental.pallas import tpu as pltpu
from jax.sharding import PartitionSpec as P

MESH = pl.DeviceIdType.MESH

FLOW = [(a, b, c) for a in (-1, 0, 1) for b in (-1, 0, 1) for c in (-1, 0, 1)]
SCAL = [(0, 0, 0), (1, 0, 0), (-1, 0, 0), (0, 1, 0), (0, -1, 0), (0, 0, 1), (0, 0, -1)]
SCAL_OPP = [0, 2, 1, 4, 3, 6, 5]
STATE = FLOW + SCAL + SCAL

ORDER = [i for a in (-1, 0, 1) for i in range(41) if STATE[i][0] == a]
SLOT = [ORDER.index(i) for i in range(41)]
LOW = (0, 11)
HIGH = (30, 41)
ROWS = [[i for i in range(41) if STATE[i][1] == b] for b in (-1, 1)]
EDGES = [(a, b) for a in (-1, 1) for b in (-1, 1)]
EDGE_FIELDS = [[i for i in range(27) if STATE[i][:2] == ab] for ab in EDGES]


def collide(load, flag, emit):
    f = [load(i) for i in range(27)]
    wall = flag == 1
    fan = flag == 2
    heater = flag == 3
    exhaust = flag == 4
    line, diff = {}, {}
    for a in range(3):
        for b in range(3):
            lo, mid, hi = f[9 * a + 3 * b], f[9 * a + 3 * b + 1], f[9 * a + 3 * b + 2]
            line[a, b] = (lo + hi) + mid
            diff[a, b] = hi - lo
    plane = [(line[a, 0] + line[a, 2]) + line[a, 1] for a in range(3)]
    rho = (plane[0] + plane[2]) + plane[1]
    mom_x = plane[2] - plane[0]
    mom_y = (line[0, 2] - line[0, 0]) + (line[2, 2] - line[2, 0]) + (line[1, 2] - line[1, 0])
    mom_z = (
        ((diff[0, 0] + diff[0, 1]) + (diff[0, 2] + diff[1, 0]))
        + ((diff[1, 1] + diff[1, 2]) + (diff[2, 0] + diff[2, 1]))
        + diff[2, 2]
    )
    inv = 1.0 / jnp.where(wall, 1.0, rho)
    ux = jnp.where(fan, 0.05, mom_x * inv)
    uy = jnp.where(fan, 0.0, mom_y * inv)
    uz = jnp.where(fan, 0.0, mom_z * inv)
    forced = fan | exhaust
    alpha = jnp.where(forced, 0.0, -0.25)
    scale = jnp.where(exhaust, 1.0, rho) * jnp.where(forced, 1.0 / 216.0, 1.25 / 216.0)
    usq = ux * ux + uy * uy + uz * uz
    v = (1.5 * ux, 1.5 * uy, 1.5 * uz)
    base1 = scale * (1.0 - 1.5 * usq)
    base = {0: 64.0 * base1, 1: 16.0 * base1, 2: 4.0 * base1, 3: base1}
    doubled = scale + scale
    q1 = tuple(doubled * t for t in v)
    q = {3: q1, 2: tuple(4.0 * t for t in q1), 1: tuple(16.0 * t for t in q1)}

    def signed(vec, direction, cache):
        if direction in cache:
            return cache[direction]
        nonzero = [n for n in range(3) if direction[n]]
        if len(nonzero) == 1:
            out = vec[nonzero[0]]
        else:
            head = list(direction)
            head[nonzero[-1]] = 0
            first = signed(vec, tuple(head), cache)
            last = vec[nonzero[-1]]
            out = first + last if direction[nonzero[-1]] > 0 else first - last
        cache[direction] = out
        return out

    vcache, qcache = {}, {1: {}, 2: {}, 3: {}}
    emit(13, jnp.where(wall, f[13], alpha * f[13] + base[0]))
    for i in range(14, 27):
        direction = FLOW[i]
        kind = sum(abs(n) for n in direction)
        odd = signed(q[kind], direction, qcache[kind])
        even = base[kind] + odd * signed(v, direction, vcache)
        opp = 26 - i
        emit(i, jnp.where(wall, f[opp], alpha * f[i] + (even + odd)))
        emit(opp, jnp.where(wall, f[i], alpha * f[opp] + (even - odd)))

    half = (0.5 * ux, 0.5 * uy, 0.5 * uz)
    factor = [0.25] + [0.125 + sign * half[n] for n in range(3) for sign in (1, -1)]
    for first, special in ((27, heater), (34, exhaust)):
        g = [load(first + j) for j in range(7)]
        total = ((g[0] + g[1]) + (g[2] + g[3])) + ((g[4] + g[5]) + g[6])
        if first == 27:
            keep = jnp.where(special, 0.0, 1.0 - 1.0 / 0.9)
            gain = jnp.where(special, 2.0, total * (1.0 / 0.9))
        else:
            keep = jnp.where(special, 0.0, 1.0 - 1.0 / 1.1)
            gain = jnp.where(special, 0.0, total * (1.0 / 1.1))
        for j in range(7):
            emit(first + j, jnp.where(wall, g[SCAL_OPP[j]], keep * g[j] + gain * factor[j]))


def exchange_kernel(
    nl, nc, nx, nk, chunks,
    pop_hbm, scal_hbm, flag_hbm, f2,
    pop, scal, flags, f1, row_out, row_in, edge_out, edge_in,
    load_sem, face_send, face_recv, row_send, row_recv, edge_send, edge_recv,
):
    me_l = lax.axis_index("loop")
    me_c = lax.axis_index("cross")
    right = lax.rem(me_l + 1, nl)
    left = lax.rem(me_l + nl - 1, nl)
    has_low = me_c > 0
    has_high = me_c < nc - 1
    has = (has_low, has_high)
    side = (me_c - 1, me_c + 1)
    around = (left, right)
    width = nk // chunks

    def loads(x):
        return (
            pltpu.make_async_copy(pop_hbm.at[:, x], pop.at[:, x], load_sem.at[0, x]),
            pltpu.make_async_copy(scal_hbm.at[:, x], scal.at[:, x], load_sem.at[1, x]),
            pltpu.make_async_copy(flag_hbm.at[x], flags.at[x], load_sem.at[2, x]),
        )

    def start_loads(x):
        for copy in loads(x):
            copy.start()

    def wait_loads(x):
        for copy in loads(x):
            copy.wait()

    start_loads(nx - 1)
    start_loads(0)

    @pl.loop(1, nx - 1)
    def _(x):
        start_loads(x)

    row_in[...] = jnp.zeros_like(row_in)
    edge_in[...] = jnp.zeros_like(edge_in)

    barrier = pltpu.get_barrier_semaphore()
    for l in around:
        pl.semaphore_signal(barrier, inc=1, device_id=(l, me_c), device_id_type=MESH)
    for s in range(2):

        @pl.when(has[s])
        def _():
            for l in (me_l,) + around:
                pl.semaphore_signal(barrier, inc=1, device_id=(l, side[s]), device_id_type=MESH)

    sides = lax.div(me_c + nc - 1, nc) + lax.div(2 * nc - 2 - me_c, nc)

    def wait_barrier():
        pl.semaphore_wait(barrier, 2 + 3 * sides)

    lane = lax.broadcasted_iota(jnp.int32, (8, 128), 1)
    first_lane = lane == 0
    last_lane = lane == 127

    def push(dst, x, k, i, value, clear):
        a, b, c = STATE[i]
        j = SLOT[i]
        if c:
            value = pltpu.roll(value, 1 if c > 0 else 127, 1)
            if clear:
                value = jnp.where(first_lane if c > 0 else last_lane, 0.0, value)
        if b == 0:
            dst[j, x + 1 + a, k + 1] = value
        elif b > 0:
            value = pltpu.roll(value, 1, 0)
            dst[j, x + 1 + a, k + 1, 1:8] = value[1:8]
            dst[j, x + 1 + a, k + 2, 0:1] = value[0:1]
        else:
            value = pltpu.roll(value, 7, 0)
            dst[j, x + 1 + a, k + 1, 0:7] = value[0:7]
            dst[j, x + 1 + a, k, 7:8] = value[7:8]

    def first_step(x, k):
        def load(i):
            return pop[i, x, k] if i < 27 else scal[i - 27, x, k]

        collide(load, flags[x, k], lambda i, v: push(f1, x, k, i, v, True))

    def second_step(x, k):
        collide(
            lambda i: f1[SLOT[i], x + 1, k + 1],
            flags[x, k],
            lambda i, v: push(f2, x, k, i, v, False),
        )

    def face(step, s, n):
        buf = (f1, f2)[step]
        lo, hi = (LOW, HIGH)[s]
        src, dst = ((0, nx), (nx + 1, 1))[s]
        rows = slice(1 + n * width, 1 + (n + 1) * width)
        return pltpu.make_async_remote_copy(
            src_ref=buf.at[lo:hi, src, rows],
            dst_ref=buf.at[lo:hi, dst, rows],
            send_sem=face_send.at[step, s, n],
            recv_sem=face_recv.at[step, s, n],
            device_id=(around[s], me_c),
            device_id_type=MESH,
        )

    def row(step, s):
        return pltpu.make_async_remote_copy(
            src_ref=row_out.at[step, s],
            dst_ref=row_in.at[step, s],
            send_sem=row_send.at[step, s],
            recv_sem=row_recv.at[step, s],
            device_id=(me_l, side[s]),
            device_id_type=MESH,
        )

    def edge(step, e):
        a, b = EDGES[e]
        return pltpu.make_async_remote_copy(
            src_ref=edge_out.at[step, e],
            dst_ref=edge_in.at[step, e],
            send_sem=edge_send.at[step, e],
            recv_sem=edge_recv.at[step, e],
            device_id=(around[(a + 1) // 2], side[(b + 1) // 2]),
            device_id_type=MESH,
        )

    def send_edges(step, s):
        buf = (f1, f2)[step]
        for e in (2 * s, 2 * s + 1):
            a, b = EDGES[e]
            for n, i in enumerate(EDGE_FIELDS[e]):
                tile, r = (nk + 1, 0) if b > 0 else (0, 7)
                x = nx + 1 if a > 0 else 0
                edge_out[step, e, n : n + 1] = buf[SLOT[i], x, tile, r : r + 1]

            @pl.when(has[(b + 1) // 2])
            def _():
                edge(step, e).start()

    def get_edges(step, s):
        buf = (f1, f2)[step]
        for e in (2 * s, 2 * s + 1):
            a, b = EDGES[e]

            @pl.when(has[1 - (b + 1) // 2])
            def _():
                edge(step, e).wait_recv()

            for n, i in enumerate(EDGE_FIELDS[e]):
                tile, r = (1, 0) if b > 0 else (nk, 7)
                x = 1 if a > 0 else nx
                buf[SLOT[i], x, tile, r : r + 1] = edge_in[step, e, n : n + 1]

    def send_rows(step):
        buf = (f1, f2)[step]
        for s in range(2):
            tile, r = ((0, 7), (nk + 1, 0))[s]
            for n, i in enumerate(ROWS[s]):
                for x in range(nx):
                    row_out[step, s, n, x : x + 1] = buf[SLOT[i], x + 1, tile, r : r + 1]

            @pl.when(has[s])
            def _():
                row(step, s).start()

    def get_rows(step):
        buf = (f1, f2)[step]
        for s in range(2):

            @pl.when(has[1 - s])
            def _():
                row(step, s).wait_recv()

            tile, r = ((nk, 7), (1, 0))[s]
            for n, i in enumerate(ROWS[s]):
                a = STATE[i][0]
                for x in range(max(a, 0), nx + min(a, 0)):
                    buf[SLOT[i], x + 1, tile, r : r + 1] = row_in[step, s, n, x : x + 1]

    for s, x in ((1, nx - 1), (0, 0)):
        wait_loads(x)

        @pl.loop(0, nk)
        def _(k):
            first_step(x, k)

        if s == 1:
            wait_barrier()
        for n in range(chunks):
            face(0, s, n).start()
        send_edges(0, s)

    @pl.loop(1, nx - 1)
    def _(x):
        wait_loads(x)

        @pl.loop(0, nk)
        def _(k):
            first_step(x, k)

    send_rows(0)

    @pl.loop(1, nx - 1)
    def _(x):
        @pl.loop(1, nk - 1)
        def _(k):
            second_step(x, k)

    get_rows(0)

    @pl.loop(1, nx - 1)
    def _(x):
        @pl.loop(0, 2)
        def _(n):
            second_step(x, n * (nk - 1))

    for n in range(chunks):
        for s, x in ((0, nx - 1), (1, 0)):
            face(0, s, n).wait_recv()
            if n == 0:
                get_edges(0, s)

            @pl.loop(n * width, (n + 1) * width)
            def _(k):
                second_step(x, k)

            if n > 0:
                face(1, 1 - s, n - 1).start()
            if n == chunks - 1:
                face(1, 1 - s, n).start()
                send_edges(1, 1 - s)

    send_rows(1)
    get_rows(1)
    for s in range(2):
        for n in range(chunks):
            face(1, s, n).wait_recv()
        get_edges(1, s)

    for step in range(2):
        for s in range(2):
            for n in range(chunks):
                face(step, s, n).wait_send()

            @pl.when(has[s])
            def _():
                row(step, s).wait_send()

        for e in range(4):

            @pl.when(has[e % 2])
            def _():
                edge(step, e).wait_send()


GROUPS = [(0, 0, 9), (11, 9, 9), (30, 18, 9)]


def store_kernel(nx, nk, f2, pop_hbm, scal_hbm, sem):
    copies = []
    for n, (slot, i, size) in enumerate(GROUPS):
        copies.append(
            pltpu.make_async_copy(
                f2.at[slot : slot + size, 1 : nx + 1, 1 : nk + 1],
                pop_hbm.at[i : i + size],
                sem.at[n],
            )
        )
    for j in range(14):
        copies.append(
            pltpu.make_async_copy(
                f2.at[SLOT[27 + j], 1 : nx + 1, 1 : nk + 1], scal_hbm.at[j], sem.at[3 + j]
            )
        )
    for copy in copies:
        copy.start()
    for copy in copies:
        copy.wait()


def per_device(nl, nc, populations, scalars, node_flags):
    nx, ny, nz = node_flags.shape
    nk = ny // 8
    chunks = 1
    f32 = jnp.float32
    padded = (41, nx + 2, nk + 2, 8, nz)
    dma = pltpu.SemaphoreType.DMA
    place = pltpu.with_memory_space_constraint
    hbm = pl.BlockSpec(memory_space=pltpu.HBM)
    vmem = pl.BlockSpec(memory_space=pltpu.VMEM)
    f2 = pl.pallas_call(
        functools.partial(exchange_kernel, nl, nc, nx, nk, chunks),
        out_shape=pltpu.VMEM(padded, f32),
        in_specs=[hbm] * 3,
        out_specs=vmem,
        scratch_shapes=[
            pltpu.VMEM((27, nx, nk, 8, nz), f32),
            pltpu.VMEM((14, nx, nk, 8, nz), f32),
            pltpu.VMEM((nx, nk, 8, nz), jnp.int32),
            pltpu.VMEM(padded, f32),
            pltpu.VMEM((2, 2, 11, nx, nz), f32),
            pltpu.VMEM((2, 2, 11, nx, nz), f32),
            pltpu.VMEM((2, 4, 8, nz), f32),
            pltpu.VMEM((2, 4, 8, nz), f32),
            dma((3, nx)),
            dma((2, 2, chunks)),
            dma((2, 2, chunks)),
            dma((2, 2)),
            dma((2, 2)),
            dma((2, 4)),
            dma((2, 4)),
        ],
        compiler_params=pltpu.CompilerParams(
            collective_id=0, has_side_effects=True, vmem_limit_bytes=40 * 2**20
        ),
    )(
        place(populations.reshape(27, nx, nk, 8, nz), pltpu.HBM),
        place(scalars.reshape(14, nx, nk, 8, nz), pltpu.HBM),
        place(node_flags.reshape(nx, nk, 8, nz), pltpu.HBM),
    )
    new_pop, new_scal = pl.pallas_call(
        functools.partial(store_kernel, nx, nk),
        out_shape=(
            jax.ShapeDtypeStruct((27, nx, nk, 8, nz), f32),
            jax.ShapeDtypeStruct((14, nx, nk, 8, nz), f32),
        ),
        in_specs=[vmem],
        out_specs=(hbm, hbm),
        scratch_shapes=[dma((17,))],
        compiler_params=pltpu.CompilerParams(vmem_limit_bytes=2**20),
    )(place(f2, pltpu.VMEM))
    return new_pop.reshape(27, nx, ny, nz), new_scal.reshape(14, nx, ny, nz)


def solution(mesh):
    wide = P(None, "loop", "cross", None)
    return jax.shard_map(
        functools.partial(per_device, mesh.shape["loop"], mesh.shape["cross"]),
        mesh=mesh,
        in_specs=(wide, wide, P("loop", "cross", None)),
        out_specs=(wide, wide),
        check_vma=False,
    )
```

time: 132 us -> 33.3 us (0.25)
  waiting for transfers between devices: 55.7 us -> 0 us
  other arithmetic: 38.9 us -> 0 us
  Pallas kernels: 0 us -> 32.6 us
  starting transfers between devices: 29.4 us -> 0 us
  local copies, waits for them, and re-layouts: 6.18 us -> 0 us
    ppermute x8 -> x0, waiting for transfers between devices: 55.7 us -> none  [the longest x4 43.6 us: padded_2(): lax.ppermute(tail, axis, [(i, (i + 1) % count) for i in range(ends)])]
    pallas_call x0 -> x2, Pallas kernels: none -> 32.6 us  [the longest x1 30.1 us: per_device(): pl.pallas_call(functools.partial(exchange_kernel, nl, nc, nx, nk, chunks)...]
    ppermute x8 -> x0, starting transfers between devices: 29.4 us -> none  [the longest x4 14.9 us: padded_2(): lax.ppermute(tail, axis, [(i, (i + 1) % count) for i in range(ends)])]
    concatenate x4 -> x0, other arithmetic: 23 us -> none  [the longest x2 22.8 us: padded_2(): jnp.concatenate([lax.ppermute(tail, axis, [(i, (i + 1) % count) for i in...]
    unnamed x100 -> x0, other arithmetic: 9.62 us -> none
    reduce_sum x3 -> x0, other arithmetic: 5.73 us -> none  [the longest x2 3.92 us: collide(): mom_x = jnp.sum(pops * table[:, 0][:, None, None, None], axis=0)]
    unnamed x54 -> x0, local copies, waits for them, and re-layouts: 5.38 us -> none
  transfers between devices with their start and end apart: 8 -> 0, of which waited for: 8 -> 0; matrix products, arithmetic and copies ran while one was open for 0% -> 0% of each run, Pallas kernels for 0% -> 0%
where the time goes in v1:
time: 33.3 us; the launch traced here: 33.2 us
  Pallas kernels  32.6 us (98%)
  between operations  0.64 us (2%)
    pallas_call x1, Pallas kernels, per_device(): pl.pallas_call(functools.partial(exchange_kernel, nl, nc, nx, nk, chunks)...  30.1 us
    pallas_call x1, Pallas kernels, per_device(): pl.pallas_call(functools.partial(store_kernel, nx, nk), out_shape=(jax.Sh...  2.5 us

profile of v1, /device:TPU:1, one launch (start us, length us, event | category | flops | bytes accessed | tf_op | source)
XLA Modules:
  0.0 33.2 jit_solution(7832035870980118950)
XLA Ops:
  0.6 30.1 %shard_map.50.f2 = f32[41,10,6,8,128]{4,3,2,1,0:T(8,128)S(1)} custom-call(f32[27,8,4,8,128]{4,3,2,1,0:T(8,128)} %bitcast.5, f32[14,8,4,8,128]{4,3,2,1,0:T(8,128)} %bitcast.6, s32[8,4,8,128]{3,2,1,0:T(8,128)} %bitcast.7), custom_call_target="tpu_custom_call" | custom-call | tf_op jit(solution)/shard_map/pallas_call | solution.py:394
  30.7 2.5 %shard_map.51 = (f32[27,8,4,8,128]{4,3,2,1,0:T(8,128)}, f32[14,8,4,8,128]{4,3,2,1,0:T(8,128)}) custom-call(f32[41,10,6,8,128]{4,3,2,1,0:T(8,128)S(1)} %shard_map.50.f2), custom_call_target="tpu_custom_call" | custom-call | tf_op jit(solution)/shard_map/pallas_call | solution.py:424

commit v2 on v1

v2 whole, which is shorter than its diff:
```python
import functools

import jax
import jax.numpy as jnp
from jax import lax
from jax.experimental import pallas as pl
from jax.experimental.pallas import tpu as pltpu
from jax.sharding import PartitionSpec as P

MESH = pl.DeviceIdType.MESH

FLOW = [(a, b, c) for a in (-1, 0, 1) for b in (-1, 0, 1) for c in (-1, 0, 1)]
SCAL = [(0, 0, 0), (1, 0, 0), (-1, 0, 0), (0, 1, 0), (0, -1, 0), (0, 0, 1), (0, 0, -1)]
SCAL_OPP = [0, 2, 1, 4, 3, 6, 5]
STATE = FLOW + SCAL + SCAL

ORDER = [i for a in (-1, 0, 1) for i in range(41) if STATE[i][0] == a]
SLOT = [ORDER.index(i) for i in range(41)]
FACE = ((0, 11), (30, 41))
ROWS = [[i for i in range(41) if STATE[i][1] == b] for b in (-1, 1)]
EDGE_FIELDS = [
    [[i for i in range(27) if STATE[i][:2] == (a, b)] for b in (-1, 1)] for a in (-1, 1)
]


def collide(load, flag, emit):
    f = [load(i) for i in range(27)]
    wall = flag == 1
    fan = flag == 2
    heater = flag == 3
    exhaust = flag == 4
    line, diff = {}, {}
    for a in range(3):
        for b in range(3):
            lo, mid, hi = f[9 * a + 3 * b], f[9 * a + 3 * b + 1], f[9 * a + 3 * b + 2]
            line[a, b] = (lo + hi) + mid
            diff[a, b] = hi - lo
    plane = [(line[a, 0] + line[a, 2]) + line[a, 1] for a in range(3)]
    rho = (plane[0] + plane[2]) + plane[1]
    mom_x = plane[2] - plane[0]
    mom_y = (line[0, 2] - line[0, 0]) + (line[2, 2] - line[2, 0]) + (line[1, 2] - line[1, 0])
    mom_z = (
        ((diff[0, 0] + diff[0, 1]) + (diff[0, 2] + diff[1, 0]))
        + ((diff[1, 1] + diff[1, 2]) + (diff[2, 0] + diff[2, 1]))
        + diff[2, 2]
    )
    inv = 1.0 / jnp.where(wall, 1.0, rho)
    ux = jnp.where(fan, 0.05, mom_x * inv)
    uy = jnp.where(fan, 0.0, mom_y * inv)
    uz = jnp.where(fan, 0.0, mom_z * inv)
    forced = fan | exhaust
    alpha = jnp.where(forced, 0.0, -0.25)
    scale = jnp.where(exhaust, 1.0, rho) * jnp.where(forced, 1.0 / 216.0, 1.25 / 216.0)
    usq = ux * ux + uy * uy + uz * uz
    v = (1.5 * ux, 1.5 * uy, 1.5 * uz)
    base1 = scale * (1.0 - 1.5 * usq)
    base = {0: 64.0 * base1, 1: 16.0 * base1, 2: 4.0 * base1, 3: base1}
    doubled = scale + scale
    q1 = tuple(doubled * t for t in v)
    q = {3: q1, 2: tuple(4.0 * t for t in q1), 1: tuple(16.0 * t for t in q1)}

    def signed(vec, direction, cache):
        if direction in cache:
            return cache[direction]
        nonzero = [n for n in range(3) if direction[n]]
        if len(nonzero) == 1:
            out = vec[nonzero[0]]
        else:
            head = list(direction)
            head[nonzero[-1]] = 0
            first = signed(vec, tuple(head), cache)
            last = vec[nonzero[-1]]
            out = first + last if direction[nonzero[-1]] > 0 else first - last
        cache[direction] = out
        return out

    vcache, qcache = {}, {1: {}, 2: {}, 3: {}}
    emit(13, jnp.where(wall, f[13], alpha * f[13] + base[0]))
    for i in range(14, 27):
        direction = FLOW[i]
        kind = sum(abs(n) for n in direction)
        odd = signed(q[kind], direction, qcache[kind])
        even = base[kind] + odd * signed(v, direction, vcache)
        opp = 26 - i
        emit(i, jnp.where(wall, f[opp], alpha * f[i] + (even + odd)))
        emit(opp, jnp.where(wall, f[i], alpha * f[opp] + (even - odd)))

    half = (0.5 * ux, 0.5 * uy, 0.5 * uz)
    factor = [0.25] + [0.125 + sign * half[n] for n in range(3) for sign in (1, -1)]
    for first, special in ((27, heater), (34, exhaust)):
        g = [load(first + j) for j in range(7)]
        total = ((g[0] + g[1]) + (g[2] + g[3])) + ((g[4] + g[5]) + g[6])
        if first == 27:
            keep = jnp.where(special, 0.0, 1.0 - 1.0 / 0.9)
            gain = jnp.where(special, 2.0, total * (1.0 / 0.9))
        else:
            keep = jnp.where(special, 0.0, 1.0 - 1.0 / 1.1)
            gain = jnp.where(special, 0.0, total * (1.0 / 1.1))
        for j in range(7):
            emit(first + j, jnp.where(wall, g[SCAL_OPP[j]], keep * g[j] + gain * factor[j]))


def exchange_kernel(
    nl, nc, nx, nk,
    pop_hbm, scal_hbm, flag_hbm, f2,
    pop, scal, flags, f1, stage, arrived, row_out, row_in, edge_out, relay, edge_in,
    load_sem, face_send, face_recv, row_send, row_recv,
    relay_send, relay_recv, edge_send, edge_recv,
):
    me_l = lax.axis_index("loop")
    me_c = lax.axis_index("cross")
    around = (lax.rem(me_l + nl - 1, nl), lax.rem(me_l + 1, nl))
    side = (me_c - 1, me_c + 1)
    has = (me_c > 0, me_c < nc - 1)
    faces = (0, nx - 1)
    pieces = ((0, 1), (nk - 1, nk), (1, nk - 1))
    inner = 2

    def loads(x):
        return (
            pltpu.make_async_copy(pop_hbm.at[:, x], pop.at[:, x], load_sem.at[0, x]),
            pltpu.make_async_copy(scal_hbm.at[:, x], scal.at[:, x], load_sem.at[1, x]),
            pltpu.make_async_copy(flag_hbm.at[x], flags.at[x], load_sem.at[2, x]),
        )

    def start_loads(x):
        for copy in loads(x):
            copy.start()

    def wait_loads(x):
        for copy in loads(x):
            copy.wait()

    start_loads(nx - 1)
    start_loads(0)

    @pl.loop(1, nx - 1)
    def _(x):
        start_loads(x)

    row_in[...] = jnp.zeros_like(row_in)
    edge_in[...] = jnp.zeros_like(edge_in)

    barrier = pltpu.get_barrier_semaphore()
    for l in around:
        pl.semaphore_signal(barrier, inc=1, device_id=(l, me_c), device_id_type=MESH)
    for t in range(2):

        @pl.when(has[t])
        def _():
            pl.semaphore_signal(barrier, inc=1, device_id=(me_l, side[t]), device_id_type=MESH)

    sides = lax.div(me_c + nc - 1, nc) + lax.div(2 * nc - 2 - me_c, nc)

    def wait_barrier():
        pl.semaphore_wait(barrier, 2 + sides)

    lane = lax.broadcasted_iota(jnp.int32, (8, 128), 1)
    first_lane = lane == 0
    last_lane = lane == 127

    def put(dst, x, k, i, value):
        b = STATE[i][1]
        j = SLOT[i]
        if b == 0:
            dst[j, x + 1, k + 1] = value
        elif b > 0:
            value = pltpu.roll(value, 1, 0)
            dst[j, x + 1, k + 1, 1:8] = value[1:8]
            dst[j, x + 1, k + 2, 0:1] = value[0:1]
        else:
            value = pltpu.roll(value, 7, 0)
            dst[j, x + 1, k + 1, 0:7] = value[0:7]
            dst[j, x + 1, k, 7:8] = value[7:8]

    def first_step(x, k):
        def load(i):
            return pop[i, x, k] if i < 27 else scal[i - 27, x, k]

        def emit(i, value):
            a, _, c = STATE[i]
            if c:
                value = pltpu.roll(value, 1 if c > 0 else 127, 1)
                value = jnp.where(first_lane if c > 0 else last_lane, 0.0, value)
            put(f1, x + a, k, i, value)

        collide(load, flags[x, k], emit)

    def second_step(x, k, s=None):
        def emit(i, value):
            a, _, c = STATE[i]
            if c:
                value = pltpu.roll(value, 1 if c > 0 else 127, 1)
            if s is not None and a == 2 * s - 1:
                stage[s, SLOT[i] - FACE[s][0], k] = value
            else:
                put(f2, x + a, k, i, value)

        collide(lambda i: f1[SLOT[i], x + 1, k + 1], flags[x, k], emit)

    def face(step, s, p):
        lo, hi = FACE[s]
        first, last = pieces[p]
        if step == 0:
            rows = slice(1 + first, 1 + last)
            src = f1.at[lo:hi, (0, nx + 1)[s], rows]
            dst = f1.at[lo:hi, (nx, 1)[s], rows]
        else:
            src = stage.at[s, :, first:last]
            dst = arrived.at[s, :, first:last]
        return pltpu.make_async_remote_copy(
            src_ref=src,
            dst_ref=dst,
            send_sem=face_send.at[step, s, p],
            recv_sem=face_recv.at[step, s, p],
            device_id=(around[s], me_c),
            device_id_type=MESH,
        )

    def row(step, t):
        return pltpu.make_async_remote_copy(
            src_ref=row_out.at[step, t],
            dst_ref=row_in.at[step, t],
            send_sem=row_send.at[step, t],
            recv_sem=row_recv.at[step, t],
            device_id=(me_l, side[t]),
            device_id_type=MESH,
        )

    def hop(s, t):
        return pltpu.make_async_remote_copy(
            src_ref=edge_out.at[0, s, t],
            dst_ref=relay.at[s, t],
            send_sem=relay_send.at[s, t],
            recv_sem=relay_recv.at[s, t],
            device_id=(around[s], me_c),
            device_id_type=MESH,
        )

    def edge(step, s, t):
        return pltpu.make_async_remote_copy(
            src_ref=relay.at[s, t] if step == 0 else edge_out.at[1, s, t],
            dst_ref=edge_in.at[step, s, t],
            send_sem=edge_send.at[step, s, t],
            recv_sem=edge_recv.at[step, s, t],
            device_id=(me_l if step == 0 else around[s], side[t]),
            device_id_type=MESH,
        )

    def send_edge(step, s, t):
        for n, i in enumerate(EDGE_FIELDS[s][t]):
            if step == 0:
                tile, r = ((0, 7), (nk + 1, 0))[t]
                value = f1[SLOT[i], (0, nx + 1)[s], tile, r : r + 1]
            else:
                tile, r = ((0, 0), (nk - 1, 7))[t]
                value = stage[s, SLOT[i] - FACE[s][0], tile, r : r + 1]
            edge_out[step, s, t, n : n + 1] = value

        @pl.when(has[t])
        def _():
            (hop(s, t) if step == 0 else edge(1, s, t)).start()

    def pass_edge(s, t):
        @pl.when(has[t])
        def _():
            hop(s, t).wait_recv()
            edge(0, s, t).start()

    def get_edge(step, s, t):
        buf = (f1, f2)[step]

        @pl.when(has[1 - t])
        def _():
            edge(step, s, t).wait_recv()

        tile, r = ((nk, 7), (1, 0))[t]
        for n, i in enumerate(EDGE_FIELDS[s][t]):
            buf[SLOT[i], (nx, 1)[s], tile, r : r + 1] = edge_in[step, s, t, n : n + 1]

    def send_row(step, t):
        buf = (f1, f2)[step]
        tile, r = ((0, 7), (nk + 1, 0))[t]
        for n, i in enumerate(ROWS[t]):
            a = STATE[i][0]
            for x in range(max(a, 0), nx + min(a, 0)):
                row_out[step, t, n, x : x + 1] = buf[SLOT[i], x + 1, tile, r : r + 1]

        @pl.when(has[t])
        def _():
            row(step, t).start()

    def get_row(step, t):
        buf = (f1, f2)[step]

        @pl.when(has[1 - t])
        def _():
            row(step, t).wait_recv()

        tile, r = ((nk, 7), (1, 0))[t]
        for n, i in enumerate(ROWS[t]):
            a = STATE[i][0]
            for x in range(max(a, 0), nx + min(a, 0)):
                buf[SLOT[i], x + 1, tile, r : r + 1] = row_in[step, t, n, x : x + 1]

    for s in (1, 0):
        wait_loads(faces[s])

        @pl.loop(0, nk)
        def _(k):
            first_step(faces[s], k)

        if s == 1:
            wait_barrier()
        for t in range(2):
            send_edge(0, s, t)
        face(0, s, inner).start()

    @pl.loop(1, nx - 1)
    def _(x):
        wait_loads(x)

        @pl.loop(0, 2)
        def _(n):
            first_step(x, n * (nk - 1))

    for t in range(2):
        send_row(0, t)
    @pl.loop(1, nx - 1)
    def _(x):
        @pl.loop(1, nk - 1)
        def _(k):
            first_step(x, k)

    for s in range(2):
        for t in range(2):
            pass_edge(s, t)
    for p in range(2):
        for s in (1, 0):
            face(0, s, p).start()

    @pl.loop(1, nx - 1)
    def _(x):
        @pl.loop(1, nk - 1)
        def _(k):
            second_step(x, k)

    for s in (1, 0):
        face(0, 1 - s, inner).wait_recv()

        @pl.loop(1, nk - 1)
        def _(k):
            second_step(faces[s], k, s)

        face(1, s, inner).start()

    for p in range(2):
        k = pieces[p][0]
        get_row(0, 1 - p)

        @pl.loop(1, nx - 1)
        def _(x):
            second_step(x, k)

        for s in (1, 0):
            face(0, 1 - s, p).wait_recv()
            get_edge(0, 1 - s, 1 - p)
            second_step(faces[s], k, s)
            send_edge(1, s, p)
        send_row(1, p)
        for s in (1, 0):
            face(1, s, p).start()

    for p in (inner, 0, 1):
        for s in range(2):
            face(1, s, p).wait_recv()

            @pl.loop(*pieces[p])
            def _(k):
                for n in range(11):
                    put(f2, (nx - 1, 0)[s], k, ORDER[FACE[s][0] + n], arrived[s, n, k])

    for t in range(2):
        get_row(1, t)
        for s in range(2):
            get_edge(1, s, t)

    for step in range(2):
        for s in range(2):
            for p in range(3):
                face(step, s, p).wait_send()
        for t in range(2):

            @pl.when(has[t])
            def _():
                row(step, t).wait_send()
                for s in range(2):
                    edge(step, s, t).wait_send()
                    if step == 0:
                        hop(s, t).wait_send()


GROUPS = [(0, 0, 9), (11, 9, 9), (30, 18, 9)]


def store_kernel(nx, nk, f2, pop_hbm, scal_hbm, sem):
    copies = []
    for n, (slot, i, size) in enumerate(GROUPS):
        copies.append(
            pltpu.make_async_copy(
                f2.at[slot : slot + size, 1 : nx + 1, 1 : nk + 1],
                pop_hbm.at[i : i + size],
                sem.at[n],
            )
        )
    for j in range(14):
        copies.append(
            pltpu.make_async_copy(
                f2.at[SLOT[27 + j], 1 : nx + 1, 1 : nk + 1], scal_hbm.at[j], sem.at[3 + j]
            )
        )
    for copy in copies:
        copy.start()
    for copy in copies:
        copy.wait()


def per_device(nl, nc, populations, scalars, node_flags):
    nx, ny, nz = node_flags.shape
    nk = ny // 8
    f32 = jnp.float32
    padded = (41, nx + 2, nk + 2, 8, nz)
    dma = pltpu.SemaphoreType.DMA
    place = pltpu.with_memory_space_constraint
    hbm = pl.BlockSpec(memory_space=pltpu.HBM)
    vmem = pl.BlockSpec(memory_space=pltpu.VMEM)
    f2 = pl.pallas_call(
        functools.partial(exchange_kernel, nl, nc, nx, nk),
        out_shape=pltpu.VMEM(padded, f32),
        in_specs=[hbm] * 3,
        out_specs=vmem,
        scratch_shapes=[
            pltpu.VMEM((27, nx, nk, 8, nz), f32),
            pltpu.VMEM((14, nx, nk, 8, nz), f32),
            pltpu.VMEM((nx, nk, 8, nz), jnp.int32),
            pltpu.VMEM(padded, f32),
            pltpu.VMEM((2, 11, nk, 8, nz), f32),
            pltpu.VMEM((2, 11, nk, 8, nz), f32),
            pltpu.VMEM((2, 2, 11, nx, nz), f32),
            pltpu.VMEM((2, 2, 11, nx, nz), f32),
            pltpu.VMEM((2, 2, 2, 8, nz), f32),
            pltpu.VMEM((2, 2, 8, nz), f32),
            pltpu.VMEM((2, 2, 2, 8, nz), f32),
            dma((3, nx)),
            dma((2, 2, 3)),
            dma((2, 2, 3)),
            dma((2, 2)),
            dma((2, 2)),
            dma((2, 2)),
            dma((2, 2)),
            dma((2, 2, 2)),
            dma((2, 2, 2)),
        ],
        compiler_params=pltpu.CompilerParams(
            collective_id=0, has_side_effects=True, vmem_limit_bytes=40 * 2**20
        ),
    )(
        place(populations.reshape(27, nx, nk, 8, nz), pltpu.HBM),
        place(scalars.reshape(14, nx, nk, 8, nz), pltpu.HBM),
        place(node_flags.reshape(nx, nk, 8, nz), pltpu.HBM),
    )
    new_pop, new_scal = pl.pallas_call(
        functools.partial(store_kernel, nx, nk),
        out_shape=(
            jax.ShapeDtypeStruct((27, nx, nk, 8, nz), f32),
            jax.ShapeDtypeStruct((14, nx, nk, 8, nz), f32),
        ),
        in_specs=[vmem],
        out_specs=(hbm, hbm),
        scratch_shapes=[dma((17,))],
        compiler_params=pltpu.CompilerParams(vmem_limit_bytes=2**20),
    )(place(f2, pltpu.VMEM))
    return new_pop.reshape(27, nx, ny, nz), new_scal.reshape(14, nx, ny, nz)


def solution(mesh):
    wide = P(None, "loop", "cross", None)
    return jax.shard_map(
        functools.partial(per_device, mesh.shape["loop"], mesh.shape["cross"]),
        mesh=mesh,
        in_specs=(wide, wide, P("loop", "cross", None)),
        out_specs=(wide, wide),
        check_vma=False,
    )
```

time: 33.3 us -> 29.8 us (0.89)
  Pallas kernels: 32.6 us -> 29.1 us
    pallas_call x1, Pallas kernels: 30.1 us -> 26.6 us  [per_device(): pl.pallas_call(functools.partial(exchange_kernel, nl, nc, nx, nk), out_sh...]
where the time goes in v2:
time: 29.8 us; the launch traced here: 29.7 us
  Pallas kernels  29.1 us (98%)
  between operations  0.64 us (2%)
    pallas_call x1, Pallas kernels, per_device(): pl.pallas_call(functools.partial(exchange_kernel, nl, nc, nx, nk), out_sh...  26.6 us
    pallas_call x1, Pallas kernels, per_device(): pl.pallas_call(functools.partial(store_kernel, nx, nk), out_shape=(jax.Sh...  2.5 us

profile of v2, /device:TPU:1, one launch (start us, length us, event | category | flops | bytes accessed | tf_op | source)
XLA Modules:
  0.0 29.7 jit_solution(437208697317825563)
XLA Ops:
  0.6 26.6 %shard_map.50.f2 = f32[41,10,6,8,128]{4,3,2,1,0:T(8,128)S(1)} custom-call(f32[27,8,4,8,128]{4,3,2,1,0:T(8,128)} %bitcast.5, f32[14,8,4,8,128]{4,3,2,1,0:T(8,128)} %bitcast.6, s32[8,4,8,128]{3,2,1,0:T(8,128)} %bitcast.7), custom_call_target="tpu_custom_call" | custom-call | tf_op jit(solution)/shard_map/pallas_call | solution.py:437
  27.2 2.5 %shard_map.51 = (f32[27,8,4,8,128]{4,3,2,1,0:T(8,128)}, f32[14,8,4,8,128]{4,3,2,1,0:T(8,128)}) custom-call(f32[41,10,6,8,128]{4,3,2,1,0:T(8,128)S(1)} %shard_map.50.f2), custom_call_target="tpu_custom_call" | custom-call | tf_op jit(solution)/shard_map/pallas_call | solution.py:472

commit v3 on v2

--- a/solution.py
+++ b/solution.py
@@ -103,9 +103,10 @@
 def exchange_kernel(
     nl, nc, nx, nk,
     pop_hbm, scal_hbm, flag_hbm, f2,
-    pop, scal, flags, f1, stage, arrived, row_out, row_in, edge_out, relay, edge_in,
+    pop, scal, flags, f1, stage, arrived, row_out, row_in,
+    hop_out, relay, relay_in, edge_out, edge_in,
     load_sem, face_send, face_recv, row_send, row_recv,
-    relay_send, relay_recv, edge_send, edge_recv,
+    hop_send, hop_recv, relay_send, relay_recv, edge_send, edge_recv,
 ):
     me_l = lax.axis_index("loop")
     me_c = lax.axis_index("cross")
@@ -113,8 +114,13 @@
     side = (me_c - 1, me_c + 1)
     has = (me_c > 0, me_c < nc - 1)
     faces = (0, nx - 1)
-    pieces = ((0, 1), (nk - 1, nk), (1, nk - 1))
-    inner = 2
+    pieces = ((0, nk // 2), (nk // 2, nk))
+    ends = (0, nk - 1)
+    behind = me_l == nl - 1
+    ahead = me_l == 0
+    level = me_l > 0
+    late = jnp.logical_and(me_c == nc // 2, level)
+    early = jnp.logical_and(me_c != nc // 2, level)
 
     def loads(x):
         return (
@@ -139,6 +145,7 @@
         start_loads(x)
 
     row_in[...] = jnp.zeros_like(row_in)
+    relay_in[...] = jnp.zeros_like(relay_in)
     edge_in[...] = jnp.zeros_like(edge_in)
 
     barrier = pltpu.get_barrier_semaphore()
@@ -227,58 +234,77 @@
             device_id_type=MESH,
         )
 
-    def hop(s, t):
+    def hop(s):
         return pltpu.make_async_remote_copy(
-            src_ref=edge_out.at[0, s, t],
-            dst_ref=relay.at[s, t],
-            send_sem=relay_send.at[s, t],
-            recv_sem=relay_recv.at[s, t],
+            src_ref=hop_out.at[s],
+            dst_ref=relay.at[s],
+            send_sem=hop_send.at[s],
+            recv_sem=hop_recv.at[s],
             device_id=(around[s], me_c),
             device_id_type=MESH,
         )
 
-    def edge(step, s, t):
+    def forward(t):
         return pltpu.make_async_remote_copy(
-            src_ref=relay.at[s, t] if step == 0 else edge_out.at[1, s, t],
-            dst_ref=edge_in.at[step, s, t],
-            send_sem=edge_send.at[step, s, t],
-            recv_sem=edge_recv.at[step, s, t],
-            device_id=(me_l if step == 0 else around[s], side[t]),
+            src_ref=relay,
+            dst_ref=relay_in.at[t],
+            send_sem=relay_send.at[t],
+            recv_sem=relay_recv.at[t],
+            device_id=(me_l, side[t]),
             device_id_type=MESH,
         )
 
-    def send_edge(step, s, t):
+    def edge(s, t):
+        return pltpu.make_async_remote_copy(
+            src_ref=edge_out.at[s, t],
+            dst_ref=edge_in.at[s, t],
+            send_sem=edge_send.at[s, t],
+            recv_sem=edge_recv.at[s, t],
+            device_id=(around[s], side[t]),
+            device_id_type=MESH,
+        )
+
+    def pack_hop(s):
+        for t in range(2):
+            tile, r = ((0, 7), (nk + 1, 0))[t]
+            for n, i in enumerate(EDGE_FIELDS[s][t]):
+                m = 3 * t + n
+                hop_out[s, m : m + 1] = f1[SLOT[i], (0, nx + 1)[s], tile, r : r + 1]
+
+    def pass_edges():
+        for s in range(2):
+            hop(s).wait_recv()
+        for t in range(2):
+
+            @pl.when(has[t])
+            def _():
+                forward(t).start()
+
+    def send_edge(s, t):
+        tile, r = ((0, 0), (nk - 1, 7))[t]
         for n, i in enumerate(EDGE_FIELDS[s][t]):
-            if step == 0:
-                tile, r = ((0, 7), (nk + 1, 0))[t]
-                value = f1[SLOT[i], (0, nx + 1)[s], tile, r : r + 1]
-            else:
-                tile, r = ((0, 0), (nk - 1, 7))[t]
-                value = stage[s, SLOT[i] - FACE[s][0], tile, r : r + 1]
-            edge_out[step, s, t, n : n + 1] = value
+            m = SLOT[i] - FACE[s][0]
+            edge_out[s, t, n : n + 1] = stage[s, m, tile, r : r + 1]
 
         @pl.when(has[t])
         def _():
-            (hop(s, t) if step == 0 else edge(1, s, t)).start()
-
-    def pass_edge(s, t):
-        @pl.when(has[t])
-        def _():
-            hop(s, t).wait_recv()
-            edge(0, s, t).start()
+            edge(s, t).start()
 
     def get_edge(step, s, t):
         buf = (f1, f2)[step]
-
-        @pl.when(has[1 - t])
-        def _():
-            edge(step, s, t).wait_recv()
+        if step == 1:
+
+            @pl.when(has[1 - t])
+            def _():
+                edge(s, t).wait_recv()
 
         tile, r = ((nk, 7), (1, 0))[t]
         for n, i in enumerate(EDGE_FIELDS[s][t]):
-            buf[SLOT[i], (nx, 1)[s], tile, r : r + 1] = edge_in[step, s, t, n : n + 1]
-
-    def send_row(step, t):
+            m = 3 * t + n
+            value = relay_in[t, s, m : m + 1] if step == 0 else edge_in[s, t, n : n + 1]
+            buf[SLOT[i], (nx, 1)[s], tile, r : r + 1] = value
+
+    def pack_row(step, t):
         buf = (f1, f2)[step]
         tile, r = ((0, 7), (nk + 1, 0))[t]
         for n, i in enumerate(ROWS[t]):
@@ -286,6 +312,7 @@
             for x in range(max(a, 0), nx + min(a, 0)):
                 row_out[step, t, n, x : x + 1] = buf[SLOT[i], x + 1, tile, r : r + 1]
 
+    def send_row(step, t):
         @pl.when(has[t])
         def _():
             row(step, t).start()
@@ -296,6 +323,8 @@
         @pl.when(has[1 - t])
         def _():
             row(step, t).wait_recv()
+            if step == 0:
+                forward(t).wait_recv()
 
         tile, r = ((nk, 7), (1, 0))[t]
         for n, i in enumerate(ROWS[t]):
@@ -303,41 +332,101 @@
             for x in range(max(a, 0), nx + min(a, 0)):
                 buf[SLOT[i], x + 1, tile, r : r + 1] = row_in[step, t, n, x : x + 1]
 
+    def both(f, *args):
+        for t in range(2):
+            f(*args, t)
+
+    def send_first(s):
+        hop(s).start()
+        face(0, s, 0).start()
+
     for s in (1, 0):
         wait_loads(faces[s])
 
-        @pl.loop(0, nk)
+        @pl.loop(0, nk, unroll=True)
         def _(k):
             first_step(faces[s], k)
 
-        if s == 1:
-            wait_barrier()
-        for t in range(2):
-            send_edge(0, s, t)
-        face(0, s, inner).start()
-
-    @pl.loop(1, nx - 1)
-    def _(x):
-        wait_loads(x)
-
-        @pl.loop(0, 2)
-        def _(n):
-            first_step(x, n * (nk - 1))
+        pack_hop(s)
+
+        @pl.when(early)
+        def _():
+            if s == 1:
+                wait_barrier()
+            send_first(s)
 
     for t in range(2):
-        send_row(0, t)
+
+        @pl.loop(1, nx - 1)
+        def _(x):
+            if t == 0:
+                wait_loads(x)
+            first_step(x, ends[t])
+
+        pack_row(0, t)
+        pl.when(early)(lambda: send_row(0, t))
+
+        @pl.when(late)
+        def _():
+            if t == 0:
+                wait_barrier()
+            send_row(0, t)
+            if t == 0:
+                for s in (1, 0):
+                    send_first(s)
+
     @pl.loop(1, nx - 1)
     def _(x):
         @pl.loop(1, nk - 1)
         def _(k):
             first_step(x, k)
 
-    for s in range(2):
-        for t in range(2):
-            pass_edge(s, t)
+    @pl.when(ahead)
+    def _():
+        wait_barrier()
+        for s in range(2):
+            send_first(s)
+        both(send_row, 0)
+        for s in range(2):
+            face(0, s, 1).start()
+
+    pass_edges()
+
+    @pl.when(level)
+    def _():
+        for s in (1, 0):
+            face(0, s, 1).start()
+
+    def outer(s, p):
+        face(0, 1 - s, p).wait_recv()
+        get_edge(0, 1 - s, 1 - p)
+
+        @pl.loop(*pieces[p], unroll=True)
+        def _(k):
+            second_step(faces[s], k, s)
+
+        send_edge(s, p)
+
+    def between(p):
+        @pl.loop(1, nx - 1)
+        def _(x):
+            second_step(x, ends[p])
+
+        pack_row(1, p)
+        send_row(1, p)
+
     for p in range(2):
-        for s in (1, 0):
-            face(0, s, p).start()
+        get_row(0, 1 - p)
+        outer(1, p)
+        face(1, 1, p).start()
+        if p == 1:
+            pl.when(behind)(lambda: face(1, 0, 0).start())
+        outer(0, p)
+        between(p)
+        if p == 0:
+            pl.when(jnp.logical_not(behind))(lambda: face(1, 0, 0).start())
+        else:
+            face(1, 0, 1).start()
 
     @pl.loop(1, nx - 1)
     def _(x):
@@ -345,33 +434,7 @@
         def _(k):
             second_step(x, k)
 
-    for s in (1, 0):
-        face(0, 1 - s, inner).wait_recv()
-
-        @pl.loop(1, nk - 1)
-        def _(k):
-            second_step(faces[s], k, s)
-
-        face(1, s, inner).start()
-
     for p in range(2):
-        k = pieces[p][0]
-        get_row(0, 1 - p)
-
-        @pl.loop(1, nx - 1)
-        def _(x):
-            second_step(x, k)
-
-        for s in (1, 0):
-            face(0, 1 - s, p).wait_recv()
-            get_edge(0, 1 - s, 1 - p)
-            second_step(faces[s], k, s)
-            send_edge(1, s, p)
-        send_row(1, p)
-        for s in (1, 0):
-            face(1, s, p).start()
-
-    for p in (inner, 0, 1):
         for s in range(2):
             face(1, s, p).wait_recv()
 
@@ -385,19 +448,19 @@
         for s in range(2):
             get_edge(1, s, t)
 
-    for step in range(2):
-        for s in range(2):
-            for p in range(3):
+    for s in range(2):
+        hop(s).wait_send()
+        for step in range(2):
+            for p in range(2):
                 face(step, s, p).wait_send()
-        for t in range(2):
-
-            @pl.when(has[t])
-            def _():
-                row(step, t).wait_send()
-                for s in range(2):
-                    edge(step, s, t).wait_send()
-                    if step == 0:
-                        hop(s, t).wait_send()
+    for t in range(2):
+
+        @pl.when(has[t])
+        def _():
+            forward(t).wait_send()
+            for s in range(2):
+                row(s, t).wait_send()
+                edge(s, t).wait_send()
 
 
 GROUPS = [(0, 0, 9), (11, 9, 9), (30, 18, 9)]
@@ -448,18 +511,22 @@
             pltpu.VMEM((2, 11, nk, 8, nz), f32),
             pltpu.VMEM((2, 2, 11, nx, nz), f32),
             pltpu.VMEM((2, 2, 11, nx, nz), f32),
-            pltpu.VMEM((2, 2, 2, 8, nz), f32),
+            pltpu.VMEM((2, 8, nz), f32),
+            pltpu.VMEM((2, 8, nz), f32),
             pltpu.VMEM((2, 2, 8, nz), f32),
-            pltpu.VMEM((2, 2, 2, 8, nz), f32),
+            pltpu.VMEM((2, 2, 8, nz), f32),
+            pltpu.VMEM((2, 2, 8, nz), f32),
             dma((3, nx)),
-            dma((2, 2, 3)),
-            dma((2, 2, 3)),
+            dma((2, 2, 2)),
+            dma((2, 2, 2)),
             dma((2, 2)),
             dma((2, 2)),
+            dma((2,)),
+            dma((2,)),
+            dma((2,)),
+            dma((2,)),
             dma((2, 2)),
             dma((2, 2)),
-            dma((2, 2, 2)),
-            dma((2, 2, 2)),
         ],
         compiler_params=pltpu.CompilerParams(
             collective_id=0, has_side_effects=True, vmem_limit_bytes=40 * 2**20

time: 29.8 us -> 29.2 us (0.980)
  Pallas kernels: 29.1 us -> 28.4 us
    pallas_call x1, Pallas kernels: 26.6 us -> 25.9 us  [per_device(): pl.pallas_call(functools.partial(exchange_kernel, nl, nc, nx, nk), out_sh...]
where the time goes in v3:
time: 29.2 us; the launch traced here: 29.1 us
  Pallas kernels  28.4 us (97%)
  between operations  0.64 us (2%)
    pallas_call x1, Pallas kernels, per_device(): pl.pallas_call(functools.partial(exchange_kernel, nl, nc, nx, nk), out_sh...  25.9 us
    pallas_call x1, Pallas kernels, per_device(): pl.pallas_call(functools.partial(store_kernel, nx, nk), out_shape=(jax.Sh...  2.5 us

profile of v3, /device:TPU:1, one launch (start us, length us, event | category | flops | bytes accessed | tf_op | source)
XLA Modules:
  0.0 29.1 jit_solution(17600522271403908379)
XLA Ops:
  0.6 25.9 %shard_map.50.f2 = f32[41,10,6,8,128]{4,3,2,1,0:T(8,128)S(1)} custom-call(f32[27,8,4,8,128]{4,3,2,1,0:T(8,128)} %bitcast.5, f32[14,8,4,8,128]{4,3,2,1,0:T(8,128)} %bitcast.6, s32[8,4,8,128]{3,2,1,0:T(8,128)} %bitcast.7), custom_call_target="tpu_custom_call" | custom-call | tf_op jit(solution)/shard_map/pallas_call | solution.py:500
  26.6 2.5 %shard_map.51 = (f32[27,8,4,8,128]{4,3,2,1,0:T(8,128)}, f32[14,8,4,8,128]{4,3,2,1,0:T(8,128)}) custom-call(f32[41,10,6,8,128]{4,3,2,1,0:T(8,128)S(1)} %shard_map.50.f2), custom_call_target="tpu_custom_call" | custom-call | tf_op jit(solution)/shard_map/pallas_call | solution.py:539

commit v4 on v3

--- a/solution.py
+++ b/solution.py
@@ -140,10 +140,6 @@
     start_loads(nx - 1)
     start_loads(0)
 
-    @pl.loop(1, nx - 1)
-    def _(x):
-        start_loads(x)
-
     row_in[...] = jnp.zeros_like(row_in)
     relay_in[...] = jnp.zeros_like(relay_in)
     edge_in[...] = jnp.zeros_like(edge_in)
@@ -156,6 +152,11 @@
         @pl.when(has[t])
         def _():
             pl.semaphore_signal(barrier, inc=1, device_id=(me_l, side[t]), device_id_type=MESH)
+
+
+    @pl.loop(1, nx - 1)
+    def _(x):
+        start_loads(x)
 
     sides = lax.div(me_c + nc - 1, nc) + lax.div(2 * nc - 2 - me_c, nc)
 
@@ -464,6 +465,7 @@
 
 
 GROUPS = [(0, 0, 9), (11, 9, 9), (30, 18, 9)]
+SCAL_GROUPS = [(SLOT[27 + j], j, size) for j, size in ((0, 1), (1, 1), (2, 1), (3, 4), (7, 1), (8, 1), (9, 1), (10, 4))]
 
 
 def store_kernel(nx, nk, f2, pop_hbm, scal_hbm, sem):
@@ -476,10 +478,12 @@
                 sem.at[n],
             )
         )
-    for j in range(14):
+    for n, (slot, j, size) in enumerate(SCAL_GROUPS):
         copies.append(
             pltpu.make_async_copy(
-                f2.at[SLOT[27 + j], 1 : nx + 1, 1 : nk + 1], scal_hbm.at[j], sem.at[3 + j]
+                f2.at[slot : slot + size, 1 : nx + 1, 1 : nk + 1],
+                scal_hbm.at[j : j + size],
+                sem.at[3 + n],
             )
         )
     for copy in copies:
@@ -544,7 +548,7 @@
         ),
         in_specs=[vmem],
         out_specs=(hbm, hbm),
-        scratch_shapes=[dma((17,))],
+        scratch_shapes=[dma((11,))],
         compiler_params=pltpu.CompilerParams(vmem_limit_bytes=2**20),
     )(place(f2, pltpu.VMEM))
     return new_pop.reshape(27, nx, ny, nz), new_scal.reshape(14, nx, ny, nz)

time: 29.2 us -> 29.1 us (level)
  no operation moved by 1% of the time
where the time goes in v4:
time: 29.1 us; the launch traced here: 28.9 us
  Pallas kernels  28.3 us (97%)
  between operations  0.64 us (2%)
    pallas_call x1, Pallas kernels, per_device(): pl.pallas_call(functools.partial(exchange_kernel, nl, nc, nx, nk), out_sh...  25.8 us
    pallas_call x1, Pallas kernels, per_device(): pl.pallas_call(functools.partial(store_kernel, nx, nk), out_shape=(jax.Sh...  2.48 us

profile of v4, /device:TPU:1, one launch (start us, length us, event | category | flops | bytes accessed | tf_op | source)
XLA Modules:
  0.0 28.9 jit_solution(15449946826099599892)
XLA Ops:
  0.6 25.8 %shard_map.50.f2 = f32[41,10,6,8,128]{4,3,2,1,0:T(8,128)S(1)} custom-call(f32[27,8,4,8,128]{4,3,2,1,0:T(8,128)} %bitcast.5, f32[14,8,4,8,128]{4,3,2,1,0:T(8,128)} %bitcast.6, s32[8,4,8,128]{3,2,1,0:T(8,128)} %bitcast.7), custom_call_target="tpu_custom_call" | custom-call | tf_op jit(solution)/shard_map/pallas_call | solution.py:504
  26.5 2.5 %shard_map.51 = (f32[27,8,4,8,128]{4,3,2,1,0:T(8,128)}, f32[14,8,4,8,128]{4,3,2,1,0:T(8,128)}) custom-call(f32[41,10,6,8,128]{4,3,2,1,0:T(8,128)S(1)} %shard_map.50.f2), custom_call_target="tpu_custom_call" | custom-call | tf_op jit(solution)/shard_map/pallas_call | solution.py:543

commit v5 on v4

--- a/solution.py
+++ b/solution.py
@@ -358,7 +358,7 @@
 
     for t in range(2):
 
-        @pl.loop(1, nx - 1)
+        @pl.loop(1, nx - 1, unroll=2)
         def _(x):
             if t == 0:
                 wait_loads(x)

time: 29.1 us -> 30 us (1.031)
  Pallas kernels: 28.3 us -> 29.2 us
    pallas_call x1, Pallas kernels: 25.8 us -> 26.7 us  [per_device(): pl.pallas_call(functools.partial(exchange_kernel, nl, nc, nx, nk), out_sh...]
where the time goes in v5:
time: 30 us; the launch traced here: 29.9 us
  Pallas kernels  29.2 us (97%)
  between operations  0.64 us (2%)
    pallas_call x1, Pallas kernels, per_device(): pl.pallas_call(functools.partial(exchange_kernel, nl, nc, nx, nk), out_sh...  26.7 us
    pallas_call x1, Pallas kernels, per_device(): pl.pallas_call(functools.partial(store_kernel, nx, nk), out_shape=(jax.Sh...  2.48 us

profile of v5, /device:TPU:1, one launch (start us, length us, event | category | flops | bytes accessed | tf_op | source)
XLA Modules:
  0.0 29.9 jit_solution(16937872925548909038)
XLA Ops:
  0.6 26.7 %shard_map.50.f2 = f32[41,10,6,8,128]{4,3,2,1,0:T(8,128)S(1)} custom-call(f32[27,8,4,8,128]{4,3,2,1,0:T(8,128)} %bitcast.5, f32[14,8,4,8,128]{4,3,2,1,0:T(8,128)} %bitcast.6, s32[8,4,8,128]{3,2,1,0:T(8,128)} %bitcast.7), custom_call_target="tpu_custom_call" | custom-call | tf_op jit(solution)/shard_map/pallas_call | solution.py:504
  27.4 2.5 %shard_map.51 = (f32[27,8,4,8,128]{4,3,2,1,0:T(8,128)}, f32[14,8,4,8,128]{4,3,2,1,0:T(8,128)}) custom-call(f32[41,10,6,8,128]{4,3,2,1,0:T(8,128)S(1)} %shard_map.50.f2), custom_call_target="tpu_custom_call" | custom-call | tf_op jit(solution)/shard_map/pallas_call | solution.py:543
